TPU v7x, 32 devices: a whole 2x2x4 slice. The times are simulated.
32 devices in a mesh: sec: 4 (over y, x), tile: 8 (over z, core).
Axes of the slice: x: 2, y: 2, z: 4, core: 2. Of those that a mesh axis runs over, the one named last changes fastest.
Arguments:
- displacement: float32 [2, 16, 256, 256], P(None, 'sec', 'tile'), may hold values from -3 to 3
- coupling: float32 [4, 16, 256, 256], P(None, 'sec', 'tile'), may hold values from 0.1 to 1
- matches: float32 [4, 2, 16, 256, 256], P(None, None, 'sec', 'tile'), may hold values from -3 to 3
- step_sizes: float32 [2, 8], replicated, may hold values from 0.1 to 0.35
- restarts: int32 [2, 8], replicated, may hold values 0 or 1
- images: float32 [4, 64, 256, 256], P('sec', 'tile'), may hold values from 0 to 1
- block_anchor: int32 [4, 64], P('sec', 'tile'), may hold values from 0 to 32767
- block_dest: int32 [4, 64, 1], P('sec', 'tile'), may hold values from 0 to 7; in each aligned block of 8 rows (0 to 7, 8 to 15, ..., all dimensions but the last counted through in order) at most 2 rows name the same one
- block_slot: int32 [4, 64], P('sec', 'tile'), may hold values from 0 to 1
- block_offset: int32 [4, 64, 2], P('sec', 'tile'), may hold values from 0 to 128
- block_count: int32 [4, 8], P('sec', 'tile'), may hold values from 6 to 8, as said below
Outputs:
- aligned: float32 [2, 16, 256, 256], P(None, 'sec', 'tile')
- spans: float32 [64, 384, 384], P(('sec', 'tile'))
Inputs may be any that keep to these rules, and one draw needn't show every extreme that they name: `block_dest`: no tile index is named by more than 2 of the block slots of one device, and 2 is reached. `block_count`: some device uses all 8 slots.
All inputs are finite; a program needn't handle non-finite values.
Results may differ from a plain program's by a relative error of at most 0.0003.
Values sent between devices are 32-bit elements; how exact they have to be, the bound alone decides.
A program may use at most 128 MiB of HBM per device.

v0:
```python
import jax
import jax.numpy as jnp
from jax import lax
from jax.sharding import PartitionSpec as P

OUTER = 2
FIRE_STEPS = 8
BPP = 256
CH = 384
SPAN_DEV = 2
STIFFNESS = 1.0
MIXING = 0.1
EPSILON = 1e-06
SPEED_CAP = 0.1
PRECISE = lax.Precision.HIGHEST


def with_halo(array, sides, width):
    for axis, dim in sides:
        size, length = (lax.axis_size(axis), array.shape[dim])
        up = [(i, (i + 1) % size) for i in range(size - 1)]
        down = [(j, i) for i, j in up]
        last = lax.slice_in_dim(array, length - width, length, axis=dim)
        leading = lax.slice_in_dim(array, 0, width, axis=dim)
        before = lax.ppermute(last, axis, up)
        after = lax.ppermute(leading, axis, down)
        array = jnp.concatenate([before, array, after], axis=dim)
    return array


def forces(current, refer, coupling, matches, first_sec, sections_all):
    strain = current - refer
    rimmed = with_halo(strain, (("tile", 2),), 1)
    sides = jnp.pad(strain, ((0, 0), (0, 0), (0, 0), (1, 1)))
    summed = STIFFNESS * (
        rimmed[:, :, 2:] + rimmed[:, :, :-2] + sides[..., 2:] + sides[..., :-2] - 4.0 * strain
    )
    stacked = with_halo(current, (("sec", 1),), 2)
    sections_dev = current.shape[1]
    section = first_sec + jnp.arange(sections_dev)
    for which_k, reach in enumerate((-2, -1, 1, 2)):
        beside = stacked[:, 2 + reach : 2 + reach + sections_dev]
        usable = ((section + reach >= 0) & (section + reach < sections_all)).astype(jnp.float32)
        summed = summed + usable[None, :, None, None] * coupling[which_k][None] * (
            beside + matches[which_k] - current
        )
    return summed


def hat_rows(shift, size, source):
    row_pos = jnp.arange(size).astype(jnp.float32)[None, :, None]
    src_pos = jnp.arange(source).astype(jnp.float32)[None, None, :]
    return jnp.maximum(0.0, 1.0 - jnp.abs(row_pos - src_pos - shift[:, None, None]))


def warp_blocks(blocks_in, shift_y, shift_x):
    row_hats = hat_rows(shift_y, CH, BPP)
    col_hats = hat_rows(shift_x, CH, BPP)
    halfway = jnp.einsum("bij,bkj->bik", blocks_in, col_hats, precision=PRECISE)
    return jnp.einsum("bri,bik->brk", row_hats, halfway, precision=PRECISE)


def body(
    displacement,
    coupling,
    matches,
    step_sizes,
    restarts,
    images,
    block_anchor,
    block_dest,
    block_slot,
    block_offset,
    block_count,
):
    sections_dev = displacement.shape[1]
    first_sec = lax.axis_index("sec") * sections_dev
    sections_all = sections_dev * lax.axis_size("sec")
    node_total = 2.0 * sections_all * displacement.shape[3] * displacement.shape[3]
    current = displacement
    refer = displacement
    velocity = jnp.zeros_like(displacement)
    for outer_step in range(OUTER):
        for inner_step in range(FIRE_STEPS):
            delta = step_sizes[outer_step, inner_step]
            push = forces(current, refer, coupling, matches, first_sec, sections_all)
            velocity = velocity + delta * push
            speed_sq, push_sq = lax.psum(
                (jnp.sum(velocity * velocity), jnp.sum(push * push)), ("sec", "tile")
            )
            ratio = jnp.sqrt(speed_sq + EPSILON) / jnp.sqrt(push_sq + EPSILON)
            limit = jnp.minimum(1.0, SPEED_CAP / jnp.sqrt(speed_sq / node_total + EPSILON))
            retain = 1.0 - restarts[outer_step, inner_step].astype(jnp.float32)
            velocity = limit * retain * ((1.0 - MIXING) * velocity + MIXING * ratio * push)
            current = current + delta * velocity
        refer = current
        velocity = jnp.zeros_like(current)
    flat_disp = current.reshape(2, -1)
    moved = jnp.take(flat_disp, block_anchor[0], axis=1)
    blocks_here = block_anchor.shape[1]
    usable = (jnp.arange(blocks_here) < block_count[0, 0]).astype(jnp.float32)
    offsets = block_offset[0].astype(jnp.float32)
    shift_y = offsets[:, 0] + moved[0]
    shift_x = offsets[:, 1] + moved[1]
    owners = block_dest[0, :, 0]
    slot_hot = (block_slot[0][:, None] == jnp.arange(SPAN_DEV)[None, :]).astype(
        jnp.float32
    ) * usable[:, None]
    tiles = lax.axis_size("tile")
    capacity = max(2, 2 * blocks_here // tiles)
    owner_hot = (owners[:, None] == jnp.arange(tiles)[None, :]).astype(jnp.int32)
    rank_all = jnp.cumsum(owner_hot, axis=0) - owner_hot
    rank_own = jnp.sum(rank_all * owner_hot, axis=1)
    position = owners * capacity + rank_own
    placer = (position[None, :] == jnp.arange(tiles * capacity)[:, None]).astype(jnp.float32)
    send_blocks = jnp.einsum("sb,bij->sij", placer, images[0], precision=PRECISE).reshape(
        tiles, capacity, BPP, BPP
    )
    shifts_both = jnp.stack([shift_y, shift_x], axis=1)
    send_shift = jnp.dot(placer, shifts_both, precision=PRECISE).reshape(tiles, capacity, 2)
    send_select = jnp.dot(placer, slot_hot, precision=PRECISE).reshape(tiles, capacity, SPAN_DEV)
    blocks_in = lax.all_to_all(send_blocks, "tile", split_axis=0, concat_axis=0, tiled=True)
    shift_in = lax.all_to_all(send_shift, "tile", split_axis=0, concat_axis=0, tiled=True)
    select_in = lax.all_to_all(send_select, "tile", split_axis=0, concat_axis=0, tiled=True)
    sources = blocks_in.shape[0]
    items = blocks_in.shape[1]
    drawn = warp_blocks(
        blocks_in.reshape(sources * items, BPP, BPP),
        shift_in[..., 0].reshape(-1),
        shift_in[..., 1].reshape(-1),
    )
    drawn = drawn.reshape(sources, items, CH, CH)
    pieces = jnp.einsum("skc,skrq->kcrq", select_in, drawn, precision=PRECISE)
    spans = jnp.sum(pieces, axis=0)
    return (current, spans)


def solution(mesh):
    placed = (
        P(None, "sec", "tile", None),
        P(None, "sec", "tile", None),
        P(None, None, "sec", "tile", None),
        P(),
        P(),
        P("sec", "tile", None, None),
        P("sec", "tile"),
        P("sec", "tile", None),
        P("sec", "tile"),
        P("sec", "tile", None),
        P("sec", "tile"),
    )
    return jax.shard_map(
        body,
        mesh=mesh,
        in_specs=placed,
        out_specs=(P(None, "sec", "tile", None), P(("sec", "tile"), None, None)),
        check_vma=False,
    )
```

profile of v0, /device:TPU:0, one launch (start us, length us, event | category | flops | bytes accessed | tf_op | source)
XLA Modules:
  0.0 1109.9 jit_solution(523799049433969451)
XLA Ops:
  1.8 4.9 collective-permute-start.2
  9.2 2.0 fusion.457
  11.8 2.0 fusion.458
  16.2 3.0 collective-permute-start.1
  20.0 3.0 multiply_reduce_fusion.30
  23.0 43.6 %all-reduce.31 = (f32[]{:T(128)}, f32[]{:T(128)}) all-reduce(f32[]{:T(128)} %get-tuple-element.41, f32[]{:T(128)} %get-tuple-element.40), channel_id=1, replica_groups=mesh['sec'=4,'tile'=8] {'sec','tile'}, use_global_device_ids=true, to_apply=%region_1.2 | all-reduce | flops 2 | bytes 16 | tf_op jit(solution)/shard_map/psum | solution.py:88
  69.4 4.2 collective-permute-start.6
  76.2 3.0 collective-permute-start.5
  81.0 2.4 multiply_reduce_fusion.28
  83.4 42.6 %all-reduce.30 = (f32[]{:T(128)}, f32[]{:T(128)}) all-reduce(f32[]{:T(128)} %get-tuple-element.39, f32[]{:T(128)} %get-tuple-element.38), channel_id=1, replica_groups=mesh['sec'=4,'tile'=8] {'sec','tile'}, use_global_device_ids=true, to_apply=%region_5.6 | all-reduce | flops 2 | bytes 16 | tf_op jit(solution)/shard_map/psum | solution.py:88
  129.3 4.2 collective-permute-start.10
  136.2 3.0 collective-permute-start.9
  142.7 41.5 %all-reduce.29 = (f32[]{:T(128)}, f32[]{:T(128)}) all-reduce(f32[]{:T(128)} %get-tuple-element.37, f32[]{:T(128)} %get-tuple-element.36), channel_id=1, replica_groups=mesh['sec'=4,'tile'=8] {'sec','tile'}, use_global_device_ids=true, to_apply=%region_9.10 | all-reduce | flops 2 | bytes 16 | tf_op jit(solution)/shard_map/psum | solution.py:88
  187.1 4.2 collective-permute-start.14
  193.9 3.0 collective-permute-start.13
  200.4 42.6 %all-reduce.28 = (f32[]{:T(128)}, f32[]{:T(128)}) all-reduce(f32[]{:T(128)} %get-tuple-element.35, f32[]{:T(128)} %get-tuple-element.34), channel_id=1, replica_groups=mesh['sec'=4,'tile'=8] {'sec','tile'}, use_global_device_ids=true, to_apply=%region_13.14 | all-reduce | flops 2 | bytes 16 | tf_op jit(solution)/shard_map/psum | solution.py:88
  245.7 4.2 collective-permute-start.18
  252.5 3.0 collective-permute-start.17
  259.0 41.5 %all-reduce.27 = (f32[]{:T(128)}, f32[]{:T(128)}) all-reduce(f32[]{:T(128)} %get-tuple-element.33, f32[]{:T(128)} %get-tuple-element.32), channel_id=1, replica_groups=mesh['sec'=4,'tile'=8] {'sec','tile'}, use_global_device_ids=true, to_apply=%region_17.18 | all-reduce | flops 2 | bytes 16 | tf_op jit(solution)/shard_map/psum | solution.py:88
  303.4 4.2 collective-permute-start.22
  310.3 3.0 collective-permute-start.21
  316.8 42.6 %all-reduce.26 = (f32[]{:T(128)}, f32[]{:T(128)}) all-reduce(f32[]{:T(128)} %get-tuple-element.31, f32[]{:T(128)} %get-tuple-element.30), channel_id=1, replica_groups=mesh['sec'=4,'tile'=8] {'sec','tile'}, use_global_device_ids=true, to_apply=%region_21.22 | all-reduce | flops 2 | bytes 16 | tf_op jit(solution)/shard_map/psum | solution.py:88
  362.2 4.2 collective-permute-start.26
  369.0 3.0 collective-permute-start.25
  375.4 41.5 %all-reduce.25 = (f32[]{:T(128)}, f32[]{:T(128)}) all-reduce(f32[]{:T(128)} %get-tuple-element.29, f32[]{:T(128)} %get-tuple-element.28), channel_id=1, replica_groups=mesh['sec'=4,'tile'=8] {'sec','tile'}, use_global_device_ids=true, to_apply=%region_25.26 | all-reduce | flops 2 | bytes 16 | tf_op jit(solution)/shard_map/psum | solution.py:88
  419.6 4.2 collective-permute-start.30
  426.4 3.2 collective-permute-start.29
  433.0 42.6 %all-reduce.24 = (f32[]{:T(128)}, f32[]{:T(128)}) all-reduce(f32[]{:T(128)} %get-tuple-element.27, f32[]{:T(128)} %get-tuple-element.26), channel_id=1, replica_groups=mesh['sec'=4,'tile'=8] {'sec','tile'}, use_global_device_ids=true, to_apply=%region_29.30 | all-reduce | flops 2 | bytes 16 | tf_op jit(solution)/shard_map/psum | solution.py:88
  478.4 4.2 collective-permute-start.34
  485.2 3.0 collective-permute-start.33
  491.6 41.4 %all-reduce.23 = (f32[]{:T(128)}, f32[]{:T(128)}) all-reduce(f32[]{:T(128)} %get-tuple-element.25, f32[]{:T(128)} %get-tuple-element.24), channel_id=1, replica_groups=mesh['sec'=4,'tile'=8] {'sec','tile'}, use_global_device_ids=true, to_apply=%region_33.34 | all-reduce | flops 2 | bytes 16 | tf_op jit(solution)/shard_map/psum | solution.py:88
  535.7 4.2 collective-permute-start.38
  542.5 3.0 collective-permute-start.37
  547.3 2.3 multiply_reduce_fusion.12
  549.6 42.6 %all-reduce.22 = (f32[]{:T(128)}, f32[]{:T(128)}) all-reduce(f32[]{:T(128)} %get-tuple-element.23, f32[]{:T(128)} %get-tuple-element.22), channel_id=1, replica_groups=mesh['sec'=4,'tile'=8] {'sec','tile'}, use_global_device_ids=true, to_apply=%region_37.38 | all-reduce | flops 2 | bytes 16 | tf_op jit(solution)/shard_map/psum | solution.py:88
  595.8 4.2 collective-permute-start.42
  602.6 3.0 collective-permute-start.41
  606.5 3.5 all-to-all-start
  612.3 42.3 %all-reduce.21 = (f32[]{:T(128)}, f32[]{:T(128)}) all-reduce(f32[]{:T(128)} %get-tuple-element.21, f32[]{:T(128)} %get-tuple-element.20), channel_id=1, replica_groups=mesh['sec'=4,'tile'=8] {'sec','tile'}, use_global_device_ids=true, to_apply=%region_41.42 | all-reduce | flops 2 | bytes 16 | tf_op jit(solution)/shard_map/psum | solution.py:88
  657.4 4.2 collective-permute-start.46
  664.2 3.0 collective-permute-start.45
  670.8 42.6 %all-reduce.20 = (f32[]{:T(128)}, f32[]{:T(128)}) all-reduce(f32[]{:T(128)} %get-tuple-element.19, f32[]{:T(128)} %get-tuple-element.18), channel_id=1, replica_groups=mesh['sec'=4,'tile'=8] {'sec','tile'}, use_global_device_ids=true, to_apply=%region_45.46 | all-reduce | flops 2 | bytes 16 | tf_op jit(solution)/shard_map/psum | solution.py:88
  716.0 4.2 collective-permute-start.50
  722.8 3.0 collective-permute-start.49
  729.3 41.5 %all-reduce.19 = (f32[]{:T(128)}, f32[]{:T(128)}) all-reduce(f32[]{:T(128)} %get-tuple-element.17, f32[]{:T(128)} %get-tuple-element.16), channel_id=1, replica_groups=mesh['sec'=4,'tile'=8] {'sec','tile'}, use_global_device_ids=true, to_apply=%region_49.50 | all-reduce | flops 2 | bytes 16 | tf_op jit(solution)/shard_map/psum | solution.py:88
  773.7 4.2 collective-permute-start.54
  780.5 3.0 collective-permute-start.53
  787.0 42.6 %all-reduce.18 = (f32[]{:T(128)}, f32[]{:T(128)}) all-reduce(f32[]{:T(128)} %get-tuple-element.15, f32[]{:T(128)} %get-tuple-element.14), channel_id=1, replica_groups=mesh['sec'=4,'tile'=8] {'sec','tile'}, use_global_device_ids=true, to_apply=%region_53.54 | all-reduce | flops 2 | bytes 16 | tf_op jit(solution)/shard_map/psum | solution.py:88
  832.4 4.2 collective-permute-start.58
  839.2 3.0 collective-permute-start.57
  845.6 41.7 %all-reduce.17 = (f32[]{:T(128)}, f32[]{:T(128)}) all-reduce(f32[]{:T(128)} %get-tuple-element.13, f32[]{:T(128)} %get-tuple-element.12), channel_id=1, replica_groups=mesh['sec'=4,'tile'=8] {'sec','tile'}, use_global_device_ids=true, to_apply=%region_57.58 | all-reduce | flops 2 | bytes 16 | tf_op jit(solution)/shard_map/psum | solution.py:88
  890.0 4.2 collective-permute-start.62
  896.8 3.0 collective-permute-start.61
  903.2 42.6 %all-reduce.16 = (f32[]{:T(128)}, f32[]{:T(128)}) all-reduce(f32[]{:T(128)} %get-tuple-element.11, f32[]{:T(128)} %get-tuple-element.10), channel_id=1, replica_groups=mesh['sec'=4,'tile'=8] {'sec','tile'}, use_global_device_ids=true, to_apply=%region_61.62 | all-reduce | flops 2 | bytes 16 | tf_op jit(solution)/shard_map/psum | solution.py:88
  948.4 8.5 copy.33
  957.0 6.3 gather_fusion
  964.4 3.5 all-to-all-start.1
  967.9 4.3 fusion.20
  972.3 3.3 copy.36
  975.5 5.1 all-to-all-start.2
  981.0 93.7 %all-to-all-done.2 = f32[8,2,256,256]{3,2,1,0:T(8,128)} async-done(((f32[8,2,256,256]{3,2,1,0:T(8,128)}), f32[8,2,256,256]{3,2,1,0:T(8,128)}, u32[]{:S(2)}, u32[]{:S(2)}) %all-to-all-start.2) | async-done | bytes 4194336 | tf_op jit(solution)/shard_map/all_to_all | solution.py:122
  1074.7 10.7 fusion.2
  1085.4 12.1 %fusion.7 = f32[16,384,384]{2,1,0:T(8,128)S(1)} fusion(f32[16,256,384]{2,1,0:T(8,128)S(1)} %fusion.2, f32[16]{0:T(128)S(1)} %sub.587, f32[384,256]{1,0:T(8,128)S(1)} %broadcast_subtract_fusion), kind=kOutput, calls=%fused_computation.8 | convolution fusion | flops 7254048768 | bytes 16121920 | tf_op jit(solution)/shard_map/bri,bik->brk/dot_general | solution.py:60
  1097.5 11.1 fusion.23
  (204 shorter events, 99.0 us)
Async XLA Ops:
  1.8 12.1 %collective-permute-start.2 = (f32[2,2,32,256]{3,2,1,0:T(8,128)S(1)}, f32[2,2,32,256]{3,2,1,0:T(8,128)S(1)}, u32[]{:S(2)}, u32[]{:S(2)}) collective-permute-start(f32[2,2,32,256]{3,2,1,0:T(8,128)S(1)} %get-tuple-element.205), channel_id=1, source_target_pairs={{0,8},{8,16},{16,24},{1,9},{9,17},{17,25},{2,10},{10,18},{18,26},{... | collective-permute-start | bytes 393224 | tf_op jit(solution)/shard_map/ppermute | solution.py:25
  6.6 12.6 %collective-permute-start.3 = (f32[2,2,32,256]{3,2,1,0:T(8,128)S(1)}, f32[2,2,32,256]{3,2,1,0:T(8,128)S(1)}, u32[]{:S(2)}, u32[]{:S(2)}) collective-permute-start(f32[2,2,32,256]{3,2,1,0:T(8,128)S(1)} %get-tuple-element.206), channel_id=1, source_target_pairs={{8,0},{16,8},{24,16},{9,1},{17,9},{25,17},{10,2},{18,10},{26,18},{... | collective-permute-start | bytes 393224 | tf_op jit(solution)/shard_map/ppermute | solution.py:26
  14.9 4.4 collective-permute-start
  16.2 3.8 collective-permute-start.1
  69.4 10.7 collective-permute-start.6
  73.6 7.4 collective-permute-start.7
  74.9 5.0 collective-permute-start.4
  76.2 3.8 collective-permute-start.5
  129.3 10.7 collective-permute-start.10
  133.5 7.4 collective-permute-start.11
  134.9 5.0 collective-permute-start.8
  136.2 3.8 collective-permute-start.9
  187.1 10.7 collective-permute-start.14
  191.3 7.5 collective-permute-start.15
  192.6 5.0 collective-permute-start.12
  193.9 3.8 collective-permute-start.13
  245.7 10.7 collective-permute-start.18
  249.9 7.4 collective-permute-start.19
  251.2 5.0 collective-permute-start.16
  252.5 3.8 collective-permute-start.17
  303.4 10.7 collective-permute-start.22
  307.6 7.5 collective-permute-start.23
  309.0 5.0 collective-permute-start.20
  310.3 3.8 collective-permute-start.21
  362.2 10.7 collective-permute-start.26
  366.4 7.5 collective-permute-start.27
  367.7 5.1 collective-permute-start.24
  369.0 3.9 collective-permute-start.25
  419.6 10.8 collective-permute-start.30
  423.8 7.4 collective-permute-start.31
  425.1 5.3 collective-permute-start.28
  426.4 4.0 collective-permute-start.29
  478.4 11.2 %collective-permute-start.34 = (f32[2,2,32,256]{3,2,1,0:T(8,128)S(1)}, f32[2,2,32,256]{3,2,1,0:T(8,128)S(1)}, u32[]{:S(2)}, u32[]{:S(2)}) collective-permute-start(f32[2,2,32,256]{3,2,1,0:T(8,128)S(1)} %get-tuple-element.172), channel_id=1, source_target_pairs={{0,8},{8,16},{16,24},{1,9},{9,17},{17,25},{2,10},{10,18},{18,26},{... | collective-permute-start | bytes 393224 | tf_op jit(solution)/shard_map/ppermute | solution.py:25
  482.6 7.4 collective-permute-start.35
  483.9 5.6 collective-permute-start.32
  485.2 4.3 collective-permute-start.33
  535.7 10.7 collective-permute-start.38
  539.9 7.4 collective-permute-start.39
  541.2 4.9 collective-permute-start.36
  542.5 3.8 collective-permute-start.37
  595.8 14.8 %collective-permute-start.42 = (f32[2,2,32,256]{3,2,1,0:T(8,128)S(1)}, f32[2,2,32,256]{3,2,1,0:T(8,128)S(1)}, u32[]{:S(2)}, u32[]{:S(2)}) collective-permute-start(f32[2,2,32,256]{3,2,1,0:T(8,128)S(1)} %get-tuple-element.164), channel_id=1, source_target_pairs={{0,8},{8,16},{16,24},{1,9},{9,17},{17,25},{2,10},{10,18},{18,26},{... | collective-permute-start | bytes 393224 | tf_op jit(solution)/shard_map/ppermute | solution.py:25
  600.0 10.6 collective-permute-start.43
  601.3 9.3 collective-permute-start.40
  602.6 8.0 collective-permute-start.41
  606.5 357.9 %all-to-all-start = ((f32[8,2,2]{2,1,0:T(2,128)}), f32[8,2,2]{2,1,0:T(2,128)S(1)}, u32[]{:S(2)}, u32[]{:S(2)}) async-start(f32[8,2,2]{2,1,0:T(2,128)} %bitcast.43), calls=%async_computation | async-start | bytes 16384 | tf_op jit(solution)/shard_map/all_to_all | solution.py:124
  657.4 10.7 collective-permute-start.46
  661.6 7.4 collective-permute-start.47
  662.9 5.0 collective-permute-start.44
  664.2 3.8 collective-permute-start.45
  716.0 10.7 collective-permute-start.50
  720.2 7.4 collective-permute-start.51
  721.5 4.9 collective-permute-start.48
  773.7 10.7 collective-permute-start.54
  777.9 7.4 collective-permute-start.55
  779.2 5.0 collective-permute-start.52
  832.4 10.7 collective-permute-start.58
  836.6 7.4 collective-permute-start.59
  837.9 5.0 collective-permute-start.56
  839.2 3.8 collective-permute-start.57
  890.0 10.7 collective-permute-start.62
  894.2 7.4 collective-permute-start.63
  895.5 5.0 collective-permute-start.60
  964.4 11.1 %all-to-all-start.1 = ((f32[8,2,2]{1,2,0:T(2,128)}), f32[8,2,2]{1,2,0:T(2,128)S(1)}, u32[]{:S(2)}, u32[]{:S(2)}) async-start(f32[8,2,2]{1,2,0:T(2,128)} %copy.34), calls=%async_computation.1 | async-start | bytes 16384 | tf_op jit(solution)/shard_map/all_to_all | solution.py:123
  975.5 99.2 %all-to-all-start.2 = ((f32[8,2,256,256]{3,2,1,0:T(8,128)}), f32[8,2,256,256]{3,2,1,0:T(8,128)}, u32[]{:S(2)}, u32[]{:S(2)}) async-start(f32[8,2,256,256]{3,2,1,0:T(8,128)} %copy.36), calls=%async_computation.2 | async-start | bytes 8388608 | tf_op jit(solution)/shard_map/all_to_all | solution.py:122
  (10 other events, 775.3 us)
where the time goes:
time: 1120 us; the launch traced here: 1110 us
  blocking collectives  676 us (60%)
  starting transfers between devices  170 us (15%)
  waiting for transfers between devices  109 us (10%)
  other arithmetic  45.2 us (4%)
  between operations  44.9 us (4%)
  matrix products  39.1 us (3%)
  local copies, waits for them, and re-layouts  26 us (2%)
    psum x16, blocking collectives, body(): lax.psum((jnp.sum(velocity * velocity), jnp.sum(push * push)), ('sec', 't...  676 us
    ppermute x32, starting transfers between devices, with_halo(): before = lax.ppermute(last, axis, up)  116 us
    all_to_all x1, waiting for transfers between devices, body(): lax.all_to_all(send_blocks, 'tile', split_axis=0, concat_axis=0, tiled=True)  93.7 us
    ppermute x32, starting transfers between devices, with_halo(): after = lax.ppermute(leading, axis, down)  41.3 us
    reduce_sum x16, other arithmetic, body(): jnp.sum(push * push)  29.4 us
  transfers between devices with their start and end apart: 67, of which 27 were waited for; matrix products, arithmetic and copies ran while one was open for 4% of the time, Pallas kernels for 0%

commit v1 on v0

--- a/solution.py
+++ b/solution.py
@@ -85,8 +85,11 @@
             delta = step_sizes[outer_step, inner_step]
             push = forces(current, refer, coupling, matches, first_sec, sections_all)
             velocity = velocity + delta * push
-            speed_sq, push_sq = lax.psum(
-                (jnp.sum(velocity * velocity), jnp.sum(push * push)), ("sec", "tile")
+            columns_manage = lambda t0, peer_axis, axis_name: lax.psum(
+                lax.psum(t0, axis_name=peer_axis), axis_name
+            )
+            speed_sq, push_sq = columns_manage(
+                (jnp.sum(velocity * velocity), jnp.sum(push * push)), "tile", "sec"
             )
             ratio = jnp.sqrt(speed_sq + EPSILON) / jnp.sqrt(push_sq + EPSILON)
             limit = jnp.minimum(1.0, SPEED_CAP / jnp.sqrt(speed_sq / node_total + EPSILON))

time: 1120 us -> 835 us (0.75)
  blocking collectives: 676 us -> 421 us
  starting transfers between devices: 170 us -> 145 us
    psum x16 -> x32, blocking collectives: 676 us -> 421 us  [the longest x16 235 us: body(): lax.psum(t0, axis_name=peer_axis)]
    ppermute x32, starting transfers between devices: 116 us -> 91.2 us  [with_halo(): before = lax.ppermute(last, axis, up)]
  transfers between devices with their start and end apart: 67 -> 67, of which waited for: 27 -> 27; matrix products, arithmetic and copies ran while one was open for 4% -> 6% of each run, Pallas kernels for 0% -> 0%
where the time goes in v1:
time: 835 us; the launch traced here: 822 us
  blocking collectives  421 us (50%)
  starting transfers between devices  145 us (17%)
  waiting for transfers between devices  101 us (12%)
  other arithmetic  45.4 us (5%)
  between operations  45.3 us (5%)
  matrix products  38.8 us (5%)
  local copies, waits for them, and re-layouts  26.1 us (3%)
    psum x16, blocking collectives, body(): lax.psum(t0, axis_name=peer_axis)  235 us
    psum x16, blocking collectives, body(): lax.psum(lax.psum(t0, axis_name=peer_axis), axis_name)  185 us
    all_to_all x1, waiting for transfers between devices, body(): lax.all_to_all(send_blocks, 'tile', split_axis=0, concat_axis=0, tiled=True)  93.6 us
    ppermute x32, starting transfers between devices, with_halo(): before = lax.ppermute(last, axis, up)  91.2 us
    ppermute x32, starting transfers between devices, with_halo(): after = lax.ppermute(leading, axis, down)  41.3 us
    reduce_sum x16, other arithmetic, body(): jnp.sum(push * push)  29.6 us
  transfers between devices with their start and end apart: 67, of which 27 were waited for; matrix products, arithmetic and copies ran while one was open for 6% of the time, Pallas kernels for 0%

profile of v1, /device:TPU:0, one launch (start us, length us, event | category | flops | bytes accessed | tf_op | source)
XLA Modules:
  0.0 822.4 jit_solution(4205719594196096988)
XLA Ops:
  1.8 4.9 collective-permute-start.2
  16.2 3.0 collective-permute-start.1
  20.0 3.0 multiply_reduce_fusion.30
  23.0 17.8 %all-reduce.31 = (f32[]{:T(128)}, f32[]{:T(128)}) all-reduce(f32[]{:T(128)} %get-tuple-element.41, f32[]{:T(128)} %get-tuple-element.40), channel_id=1, replica_groups=mesh['sec'=4,'tile'=8] {'tile'}, use_global_device_ids=true, to_apply=%region_1.2 | all-reduce | flops 2 | bytes 16 | tf_op jit(solution)/shard_map/psum | solution.py:89
  40.8 11.7 %all-reduce.47 = (f32[]{:T(128)}, f32[]{:T(128)}) all-reduce(f32[]{:T(128)} %get-tuple-element.76, f32[]{:T(128)} %get-tuple-element.77), channel_id=1, replica_groups=mesh['sec'=4,'tile'=8] {'sec'}, use_global_device_ids=true, to_apply=%region_2.3 | all-reduce | flops 2 | bytes 16 | tf_op jit(solution)/shard_map/psum | solution.py:88
  60.5 3.0 collective-permute-start.5
  67.1 14.3 %all-reduce.30 = (f32[]{:T(128)}, f32[]{:T(128)}) all-reduce(f32[]{:T(128)} %get-tuple-element.39, f32[]{:T(128)} %get-tuple-element.38), channel_id=1, replica_groups=mesh['sec'=4,'tile'=8] {'tile'}, use_global_device_ids=true, to_apply=%region_7.8 | all-reduce | flops 2 | bytes 16 | tf_op jit(solution)/shard_map/psum | solution.py:89
  81.3 11.6 %all-reduce.46 = (f32[]{:T(128)}, f32[]{:T(128)}) all-reduce(f32[]{:T(128)} %get-tuple-element.74, f32[]{:T(128)} %get-tuple-element.75), channel_id=1, replica_groups=mesh['sec'=4,'tile'=8] {'sec'}, use_global_device_ids=true, to_apply=%region_8.9 | all-reduce | flops 2 | bytes 16 | tf_op jit(solution)/shard_map/psum | solution.py:88
  101.6 3.0 collective-permute-start.9
  107.6 14.3 %all-reduce.29 = (f32[]{:T(128)}, f32[]{:T(128)}) all-reduce(f32[]{:T(128)} %get-tuple-element.37, f32[]{:T(128)} %get-tuple-element.36), channel_id=1, replica_groups=mesh['sec'=4,'tile'=8] {'tile'}, use_global_device_ids=true, to_apply=%region_13.14 | all-reduce | flops 2 | bytes 16 | tf_op jit(solution)/shard_map/psum | solution.py:89
  121.8 11.6 %all-reduce.45 = (f32[]{:T(128)}, f32[]{:T(128)}) all-reduce(f32[]{:T(128)} %get-tuple-element.72, f32[]{:T(128)} %get-tuple-element.73), channel_id=1, replica_groups=mesh['sec'=4,'tile'=8] {'sec'}, use_global_device_ids=true, to_apply=%region_14.15 | all-reduce | flops 2 | bytes 16 | tf_op jit(solution)/shard_map/psum | solution.py:88
  141.5 3.0 collective-permute-start.13
  147.4 14.3 %all-reduce.28 = (f32[]{:T(128)}, f32[]{:T(128)}) all-reduce(f32[]{:T(128)} %get-tuple-element.35, f32[]{:T(128)} %get-tuple-element.34), channel_id=1, replica_groups=mesh['sec'=4,'tile'=8] {'tile'}, use_global_device_ids=true, to_apply=%region_19.20 | all-reduce | flops 2 | bytes 16 | tf_op jit(solution)/shard_map/psum | solution.py:89
  161.7 11.6 %all-reduce.44 = (f32[]{:T(128)}, f32[]{:T(128)}) all-reduce(f32[]{:T(128)} %get-tuple-element.70, f32[]{:T(128)} %get-tuple-element.71), channel_id=1, replica_groups=mesh['sec'=4,'tile'=8] {'sec'}, use_global_device_ids=true, to_apply=%region_20.21 | all-reduce | flops 2 | bytes 16 | tf_op jit(solution)/shard_map/psum | solution.py:88
  181.4 3.0 collective-permute-start.17
  187.2 14.2 %all-reduce.27 = (f32[]{:T(128)}, f32[]{:T(128)}) all-reduce(f32[]{:T(128)} %get-tuple-element.33, f32[]{:T(128)} %get-tuple-element.32), channel_id=1, replica_groups=mesh['sec'=4,'tile'=8] {'tile'}, use_global_device_ids=true, to_apply=%region_25.26 | all-reduce | flops 2 | bytes 16 | tf_op jit(solution)/shard_map/psum | solution.py:89
  201.5 11.6 %all-reduce.43 = (f32[]{:T(128)}, f32[]{:T(128)}) all-reduce(f32[]{:T(128)} %get-tuple-element.68, f32[]{:T(128)} %get-tuple-element.69), channel_id=1, replica_groups=mesh['sec'=4,'tile'=8] {'sec'}, use_global_device_ids=true, to_apply=%region_26.27 | all-reduce | flops 2 | bytes 16 | tf_op jit(solution)/shard_map/psum | solution.py:88
  220.9 3.0 collective-permute-start.21
  226.8 14.3 %all-reduce.26 = (f32[]{:T(128)}, f32[]{:T(128)}) all-reduce(f32[]{:T(128)} %get-tuple-element.31, f32[]{:T(128)} %get-tuple-element.30), channel_id=1, replica_groups=mesh['sec'=4,'tile'=8] {'tile'}, use_global_device_ids=true, to_apply=%region_31.32 | all-reduce | flops 2 | bytes 16 | tf_op jit(solution)/shard_map/psum | solution.py:89
  241.1 11.6 %all-reduce.42 = (f32[]{:T(128)}, f32[]{:T(128)}) all-reduce(f32[]{:T(128)} %get-tuple-element.66, f32[]{:T(128)} %get-tuple-element.67), channel_id=1, replica_groups=mesh['sec'=4,'tile'=8] {'sec'}, use_global_device_ids=true, to_apply=%region_32.33 | all-reduce | flops 2 | bytes 16 | tf_op jit(solution)/shard_map/psum | solution.py:88
  260.7 3.0 collective-permute-start.25
  266.6 14.3 %all-reduce.25 = (f32[]{:T(128)}, f32[]{:T(128)}) all-reduce(f32[]{:T(128)} %get-tuple-element.29, f32[]{:T(128)} %get-tuple-element.28), channel_id=1, replica_groups=mesh['sec'=4,'tile'=8] {'tile'}, use_global_device_ids=true, to_apply=%region_37.38 | all-reduce | flops 2 | bytes 16 | tf_op jit(solution)/shard_map/psum | solution.py:89
  280.9 11.6 %all-reduce.41 = (f32[]{:T(128)}, f32[]{:T(128)}) all-reduce(f32[]{:T(128)} %get-tuple-element.64, f32[]{:T(128)} %get-tuple-element.65), channel_id=1, replica_groups=mesh['sec'=4,'tile'=8] {'sec'}, use_global_device_ids=true, to_apply=%region_38.39 | all-reduce | flops 2 | bytes 16 | tf_op jit(solution)/shard_map/psum | solution.py:88
  300.4 3.0 collective-permute-start.29
  306.4 14.3 %all-reduce.24 = (f32[]{:T(128)}, f32[]{:T(128)}) all-reduce(f32[]{:T(128)} %get-tuple-element.27, f32[]{:T(128)} %get-tuple-element.26), channel_id=1, replica_groups=mesh['sec'=4,'tile'=8] {'tile'}, use_global_device_ids=true, to_apply=%region_43.44 | all-reduce | flops 2 | bytes 16 | tf_op jit(solution)/shard_map/psum | solution.py:89
  320.7 11.6 %all-reduce.40 = (f32[]{:T(128)}, f32[]{:T(128)}) all-reduce(f32[]{:T(128)} %get-tuple-element.62, f32[]{:T(128)} %get-tuple-element.63), channel_id=1, replica_groups=mesh['sec'=4,'tile'=8] {'sec'}, use_global_device_ids=true, to_apply=%region_44.45 | all-reduce | flops 2 | bytes 16 | tf_op jit(solution)/shard_map/psum | solution.py:88
  340.1 3.0 collective-permute-start.33
  346.1 14.3 %all-reduce.23 = (f32[]{:T(128)}, f32[]{:T(128)}) all-reduce(f32[]{:T(128)} %get-tuple-element.25, f32[]{:T(128)} %get-tuple-element.24), channel_id=1, replica_groups=mesh['sec'=4,'tile'=8] {'tile'}, use_global_device_ids=true, to_apply=%region_49.50 | all-reduce | flops 2 | bytes 16 | tf_op jit(solution)/shard_map/psum | solution.py:89
  360.4 11.6 %all-reduce.39 = (f32[]{:T(128)}, f32[]{:T(128)}) all-reduce(f32[]{:T(128)} %get-tuple-element.60, f32[]{:T(128)} %get-tuple-element.61), channel_id=1, replica_groups=mesh['sec'=4,'tile'=8] {'sec'}, use_global_device_ids=true, to_apply=%region_50.51 | all-reduce | flops 2 | bytes 16 | tf_op jit(solution)/shard_map/psum | solution.py:88
  379.8 3.0 collective-permute-start.37
  386.4 14.2 %all-reduce.22 = (f32[]{:T(128)}, f32[]{:T(128)}) all-reduce(f32[]{:T(128)} %get-tuple-element.23, f32[]{:T(128)} %get-tuple-element.22), channel_id=1, replica_groups=mesh['sec'=4,'tile'=8] {'tile'}, use_global_device_ids=true, to_apply=%region_55.56 | all-reduce | flops 2 | bytes 16 | tf_op jit(solution)/shard_map/psum | solution.py:89
  400.6 11.6 %all-reduce.38 = (f32[]{:T(128)}, f32[]{:T(128)}) all-reduce(f32[]{:T(128)} %get-tuple-element.58, f32[]{:T(128)} %get-tuple-element.59), channel_id=1, replica_groups=mesh['sec'=4,'tile'=8] {'sec'}, use_global_device_ids=true, to_apply=%region_56.57 | all-reduce | flops 2 | bytes 16 | tf_op jit(solution)/shard_map/psum | solution.py:88
  415.6 2.6 collective-permute-start.42
  420.8 3.0 collective-permute-start.41
  424.7 3.5 all-to-all-start
  430.5 17.7 %all-reduce.21 = (f32[]{:T(128)}, f32[]{:T(128)}) all-reduce(f32[]{:T(128)} %get-tuple-element.21, f32[]{:T(128)} %get-tuple-element.20), channel_id=1, replica_groups=mesh['sec'=4,'tile'=8] {'tile'}, use_global_device_ids=true, to_apply=%region_61.62 | all-reduce | flops 2 | bytes 16 | tf_op jit(solution)/shard_map/psum | solution.py:89
  448.2 11.6 %all-reduce.37 = (f32[]{:T(128)}, f32[]{:T(128)}) all-reduce(f32[]{:T(128)} %get-tuple-element.56, f32[]{:T(128)} %get-tuple-element.57), channel_id=1, replica_groups=mesh['sec'=4,'tile'=8] {'sec'}, use_global_device_ids=true, to_apply=%region_62.63 | all-reduce | flops 2 | bytes 16 | tf_op jit(solution)/shard_map/psum | solution.py:88
  467.7 3.0 collective-permute-start.45
  473.7 14.3 %all-reduce.20 = (f32[]{:T(128)}, f32[]{:T(128)}) all-reduce(f32[]{:T(128)} %get-tuple-element.19, f32[]{:T(128)} %get-tuple-element.18), channel_id=1, replica_groups=mesh['sec'=4,'tile'=8] {'tile'}, use_global_device_ids=true, to_apply=%region_67.68 | all-reduce | flops 2 | bytes 16 | tf_op jit(solution)/shard_map/psum | solution.py:89
  488.0 11.6 %all-reduce.36 = (f32[]{:T(128)}, f32[]{:T(128)}) all-reduce(f32[]{:T(128)} %get-tuple-element.54, f32[]{:T(128)} %get-tuple-element.55), channel_id=1, replica_groups=mesh['sec'=4,'tile'=8] {'sec'}, use_global_device_ids=true, to_apply=%region_68.69 | all-reduce | flops 2 | bytes 16 | tf_op jit(solution)/shard_map/psum | solution.py:88
  502.4 2.6 collective-permute-start.50
  507.7 3.0 collective-permute-start.49
  513.6 14.3 %all-reduce.19 = (f32[]{:T(128)}, f32[]{:T(128)}) all-reduce(f32[]{:T(128)} %get-tuple-element.17, f32[]{:T(128)} %get-tuple-element.16), channel_id=1, replica_groups=mesh['sec'=4,'tile'=8] {'tile'}, use_global_device_ids=true, to_apply=%region_73.74 | all-reduce | flops 2 | bytes 16 | tf_op jit(solution)/shard_map/psum | solution.py:89
  527.9 11.6 %all-reduce.35 = (f32[]{:T(128)}, f32[]{:T(128)}) all-reduce(f32[]{:T(128)} %get-tuple-element.52, f32[]{:T(128)} %get-tuple-element.53), channel_id=1, replica_groups=mesh['sec'=4,'tile'=8] {'sec'}, use_global_device_ids=true, to_apply=%region_74.75 | all-reduce | flops 2 | bytes 16 | tf_op jit(solution)/shard_map/psum | solution.py:88
  547.3 3.0 collective-permute-start.53
  553.2 14.2 %all-reduce.18 = (f32[]{:T(128)}, f32[]{:T(128)}) all-reduce(f32[]{:T(128)} %get-tuple-element.15, f32[]{:T(128)} %get-tuple-element.14), channel_id=1, replica_groups=mesh['sec'=4,'tile'=8] {'tile'}, use_global_device_ids=true, to_apply=%region_79.80 | all-reduce | flops 2 | bytes 16 | tf_op jit(solution)/shard_map/psum | solution.py:89
  567.5 11.6 %all-reduce.34 = (f32[]{:T(128)}, f32[]{:T(128)}) all-reduce(f32[]{:T(128)} %get-tuple-element.50, f32[]{:T(128)} %get-tuple-element.51), channel_id=1, replica_groups=mesh['sec'=4,'tile'=8] {'sec'}, use_global_device_ids=true, to_apply=%region_80.81 | all-reduce | flops 2 | bytes 16 | tf_op jit(solution)/shard_map/psum | solution.py:88
  581.8 2.6 collective-permute-start.58
  587.0 3.0 collective-permute-start.57
  592.9 14.3 %all-reduce.17 = (f32[]{:T(128)}, f32[]{:T(128)}) all-reduce(f32[]{:T(128)} %get-tuple-element.13, f32[]{:T(128)} %get-tuple-element.12), channel_id=1, replica_groups=mesh['sec'=4,'tile'=8] {'tile'}, use_global_device_ids=true, to_apply=%region_85.86 | all-reduce | flops 2 | bytes 16 | tf_op jit(solution)/shard_map/psum | solution.py:89
  607.2 11.5 %all-reduce.33 = (f32[]{:T(128)}, f32[]{:T(128)}) all-reduce(f32[]{:T(128)} %get-tuple-element.48, f32[]{:T(128)} %get-tuple-element.49), channel_id=1, replica_groups=mesh['sec'=4,'tile'=8] {'sec'}, use_global_device_ids=true, to_apply=%region_86.87 | all-reduce | flops 2 | bytes 16 | tf_op jit(solution)/shard_map/psum | solution.py:88
  626.6 3.0 collective-permute-start.61
  632.5 14.2 %all-reduce.16 = (f32[]{:T(128)}, f32[]{:T(128)}) all-reduce(f32[]{:T(128)} %get-tuple-element.11, f32[]{:T(128)} %get-tuple-element.10), channel_id=1, replica_groups=mesh['sec'=4,'tile'=8] {'tile'}, use_global_device_ids=true, to_apply=%region_91.92 | all-reduce | flops 2 | bytes 16 | tf_op jit(solution)/shard_map/psum | solution.py:89
  646.7 11.5 %all-reduce.32 = (f32[]{:T(128)}, f32[]{:T(128)}) all-reduce(f32[]{:T(128)} %get-tuple-element.46, f32[]{:T(128)} %get-tuple-element.47), channel_id=1, replica_groups=mesh['sec'=4,'tile'=8] {'sec'}, use_global_device_ids=true, to_apply=%region_92.93 | all-reduce | flops 2 | bytes 16 | tf_op jit(solution)/shard_map/psum | solution.py:88
  661.0 8.6 %copy.33 = f32[2,4,32,256]{0,3,2,1:T(8,128)} copy(f32[2,4,32,256]{3,2,1,0:T(8,128)S(1)} %multiply_add_fusion) | data formatting | bytes 524288 | tf_op jit(solution)/shard_map/add | solution.py:98
  669.7 6.3 gather_fusion
  677.1 3.3 all-to-all-start.1
  680.4 4.3 fusion.20
  684.8 3.3 copy.36
  688.0 5.3 all-to-all-start.2
  693.8 93.6 %all-to-all-done.2 = f32[8,2,256,256]{3,2,1,0:T(8,128)} async-done(((f32[8,2,256,256]{3,2,1,0:T(8,128)}), f32[8,2,256,256]{3,2,1,0:T(8,128)}, u32[]{:S(2)}, u32[]{:S(2)}) %all-to-all-start.2) | async-done | bytes 4194336 | tf_op jit(solution)/shard_map/all_to_all | solution.py:125
  787.4 10.3 %fusion.2 = f32[16,256,384]{2,1,0:T(8,128)S(1)} fusion(f32[16,256,256]{2,1,0:T(8,128)} %bitcast.55, f32[16]{0:T(128)S(1)} %sub.591, f32[384,256]{1,0:T(8,128)S(1)} %broadcast_subtract_fusion), kind=kOutput, calls=%fused_computation.3 | convolution fusion | flops 4838129664 | bytes 10879040 | tf_op jit(solution)/shard_map/bij,bkj->bik/dot_general | solution.py:59
  797.7 12.1 %fusion.7 = f32[16,384,384]{2,1,0:T(8,128)S(1)} fusion(f32[16,256,384]{2,1,0:T(8,128)S(1)} %fusion.2, f32[16]{0:T(128)S(1)} %sub.587, f32[384,256]{1,0:T(8,128)S(1)} %broadcast_subtract_fusion), kind=kOutput, calls=%fused_computation.8 | convolution fusion | flops 7254048768 | bytes 16121920 | tf_op jit(solution)/shard_map/bri,bik->brk/dot_general | solution.py:60
  809.7 11.2 %fusion.23 = f32[2,384,384]{2,0,1:T(2,128)S(1)} fusion(f32[8,2,384,384]{3,2,1,0:T(8,128)S(1)} %bitcast.214, f32[8,2,2]{0,2,1:T(2,128)S(1)} %copy.37), kind=kOutput, calls=%fused_computation.24 | convolution fusion | flops 56623104 | bytes 10616960 | tf_op jit(solution)/shard_map/skc,skrq->kcrq/dot_general | solution.py:136
  (220 shorter events, 130.4 us)
Async XLA Ops:
  1.8 12.0 %collective-permute-start.2 = (f32[2,2,32,256]{3,2,1,0:T(8,128)S(1)}, f32[2,2,32,256]{3,2,1,0:T(8,128)S(1)}, u32[]{:S(2)}, u32[]{:S(2)}) collective-permute-start(f32[2,2,32,256]{3,2,1,0:T(8,128)S(1)} %get-tuple-element.237), channel_id=1, source_target_pairs={{0,8},{8,16},{16,24},{1,9},{9,17},{17,25},{2,10},{10,18},{18,26},{... | collective-permute-start | bytes 393224 | tf_op jit(solution)/shard_map/ppermute | solution.py:25
  6.6 12.6 %collective-permute-start.3 = (f32[2,2,32,256]{3,2,1,0:T(8,128)S(1)}, f32[2,2,32,256]{3,2,1,0:T(8,128)S(1)}, u32[]{:S(2)}, u32[]{:S(2)}) collective-permute-start(f32[2,2,32,256]{3,2,1,0:T(8,128)S(1)} %get-tuple-element.238), channel_id=1, source_target_pairs={{8,0},{16,8},{24,16},{9,1},{17,9},{25,17},{10,2},{18,10},{26,18},{... | collective-permute-start | bytes 393224 | tf_op jit(solution)/shard_map/ppermute | solution.py:26
  14.9 4.4 collective-permute-start
  16.2 3.8 collective-permute-start.1
  55.4 8.9 %collective-permute-start.6 = (f32[2,2,32,256]{3,2,1,0:T(8,128)S(1)}, f32[2,2,32,256]{3,2,1,0:T(8,128)S(1)}, u32[]{:S(2)}, u32[]{:S(2)}) collective-permute-start(f32[2,2,32,256]{3,2,1,0:T(8,128)S(1)} %get-tuple-element.232), channel_id=1, source_target_pairs={{0,8},{8,16},{16,24},{1,9},{9,17},{17,25},{2,10},{10,18},{18,26},{... | collective-permute-start | bytes 393224 | tf_op jit(solution)/shard_map/ppermute | solution.py:25
  57.9 6.9 collective-permute-start.7
  59.2 5.0 collective-permute-start.4
  60.5 3.8 collective-permute-start.5
  96.4 9.1 %collective-permute-start.10 = (f32[2,2,32,256]{3,2,1,0:T(8,128)S(1)}, f32[2,2,32,256]{3,2,1,0:T(8,128)S(1)}, u32[]{:S(2)}, u32[]{:S(2)}) collective-permute-start(f32[2,2,32,256]{3,2,1,0:T(8,128)S(1)} %get-tuple-element.228), channel_id=1, source_target_pairs={{0,8},{8,16},{16,24},{1,9},{9,17},{17,25},{2,10},{10,18},{18,26},{... | collective-permute-start | bytes 393224 | tf_op jit(solution)/shard_map/ppermute | solution.py:25
  99.0 6.9 collective-permute-start.11
  100.3 5.0 collective-permute-start.8
  101.6 3.8 collective-permute-start.9
  136.4 9.0 %collective-permute-start.14 = (f32[2,2,32,256]{3,2,1,0:T(8,128)S(1)}, f32[2,2,32,256]{3,2,1,0:T(8,128)S(1)}, u32[]{:S(2)}, u32[]{:S(2)}) collective-permute-start(f32[2,2,32,256]{3,2,1,0:T(8,128)S(1)} %get-tuple-element.224), channel_id=1, source_target_pairs={{0,8},{8,16},{16,24},{1,9},{9,17},{17,25},{2,10},{10,18},{18,26},{... | collective-permute-start | bytes 393224 | tf_op jit(solution)/shard_map/ppermute | solution.py:25
  138.9 6.9 collective-permute-start.15
  140.2 5.0 collective-permute-start.12
  141.5 3.8 collective-permute-start.13
  176.2 9.1 %collective-permute-start.18 = (f32[2,2,32,256]{3,2,1,0:T(8,128)S(1)}, f32[2,2,32,256]{3,2,1,0:T(8,128)S(1)}, u32[]{:S(2)}, u32[]{:S(2)}) collective-permute-start(f32[2,2,32,256]{3,2,1,0:T(8,128)S(1)} %get-tuple-element.220), channel_id=1, source_target_pairs={{0,8},{8,16},{16,24},{1,9},{9,17},{17,25},{2,10},{10,18},{18,26},{... | collective-permute-start | bytes 393224 | tf_op jit(solution)/shard_map/ppermute | solution.py:25
  178.8 6.9 collective-permute-start.19
  180.1 5.0 collective-permute-start.16
  181.4 3.8 collective-permute-start.17
  215.7 9.0 %collective-permute-start.22 = (f32[2,2,32,256]{3,2,1,0:T(8,128)S(1)}, f32[2,2,32,256]{3,2,1,0:T(8,128)S(1)}, u32[]{:S(2)}, u32[]{:S(2)}) collective-permute-start(f32[2,2,32,256]{3,2,1,0:T(8,128)S(1)} %get-tuple-element.216), channel_id=1, source_target_pairs={{0,8},{8,16},{16,24},{1,9},{9,17},{17,25},{2,10},{10,18},{18,26},{... | collective-permute-start | bytes 393224 | tf_op jit(solution)/shard_map/ppermute | solution.py:25
  218.2 6.9 collective-permute-start.23
  219.6 4.9 collective-permute-start.20
  220.9 3.8 collective-permute-start.21
  255.5 9.1 %collective-permute-start.26 = (f32[2,2,32,256]{3,2,1,0:T(8,128)S(1)}, f32[2,2,32,256]{3,2,1,0:T(8,128)S(1)}, u32[]{:S(2)}, u32[]{:S(2)}) collective-permute-start(f32[2,2,32,256]{3,2,1,0:T(8,128)S(1)} %get-tuple-element.212), channel_id=1, source_target_pairs={{0,8},{8,16},{16,24},{1,9},{9,17},{17,25},{2,10},{10,18},{18,26},{... | collective-permute-start | bytes 393224 | tf_op jit(solution)/shard_map/ppermute | solution.py:25
  258.1 6.9 collective-permute-start.27
  259.4 5.1 collective-permute-start.24
  260.7 3.8 collective-permute-start.25
  295.3 9.0 %collective-permute-start.30 = (f32[2,2,32,256]{3,2,1,0:T(8,128)S(1)}, f32[2,2,32,256]{3,2,1,0:T(8,128)S(1)}, u32[]{:S(2)}, u32[]{:S(2)}) collective-permute-start(f32[2,2,32,256]{3,2,1,0:T(8,128)S(1)} %get-tuple-element.208), channel_id=1, source_target_pairs={{0,8},{8,16},{16,24},{1,9},{9,17},{17,25},{2,10},{10,18},{18,26},{... | collective-permute-start | bytes 393224 | tf_op jit(solution)/shard_map/ppermute | solution.py:25
  297.8 6.9 collective-permute-start.31
  299.1 5.1 collective-permute-start.28
  300.4 3.8 collective-permute-start.29
  334.9 9.6 %collective-permute-start.34 = (f32[2,2,32,256]{3,2,1,0:T(8,128)S(1)}, f32[2,2,32,256]{3,2,1,0:T(8,128)S(1)}, u32[]{:S(2)}, u32[]{:S(2)}) collective-permute-start(f32[2,2,32,256]{3,2,1,0:T(8,128)S(1)} %get-tuple-element.204), channel_id=1, source_target_pairs={{0,8},{8,16},{16,24},{1,9},{9,17},{17,25},{2,10},{10,18},{18,26},{... | collective-permute-start | bytes 393224 | tf_op jit(solution)/shard_map/ppermute | solution.py:25
  337.5 7.0 collective-permute-start.35
  338.8 5.6 collective-permute-start.32
  340.1 4.3 collective-permute-start.33
  374.7 9.0 %collective-permute-start.38 = (f32[2,2,32,256]{3,2,1,0:T(8,128)S(1)}, f32[2,2,32,256]{3,2,1,0:T(8,128)S(1)}, u32[]{:S(2)}, u32[]{:S(2)}) collective-permute-start(f32[2,2,32,256]{3,2,1,0:T(8,128)S(1)} %get-tuple-element.200), channel_id=1, source_target_pairs={{0,8},{8,16},{16,24},{1,9},{9,17},{17,25},{2,10},{10,18},{18,26},{... | collective-permute-start | bytes 393224 | tf_op jit(solution)/shard_map/ppermute | solution.py:25
  377.2 6.9 collective-permute-start.39
  378.5 5.0 collective-permute-start.36
  379.8 3.8 collective-permute-start.37
  415.6 13.1 %collective-permute-start.42 = (f32[2,2,32,256]{3,2,1,0:T(8,128)S(1)}, f32[2,2,32,256]{3,2,1,0:T(8,128)S(1)}, u32[]{:S(2)}, u32[]{:S(2)}) collective-permute-start(f32[2,2,32,256]{3,2,1,0:T(8,128)S(1)} %get-tuple-element.196), channel_id=1, source_target_pairs={{0,8},{8,16},{16,24},{1,9},{9,17},{17,25},{2,10},{10,18},{18,26},{... | collective-permute-start | bytes 393224 | tf_op jit(solution)/shard_map/ppermute | solution.py:25
  418.2 10.5 %collective-permute-start.43 = (f32[2,2,32,256]{3,2,1,0:T(8,128)S(1)}, f32[2,2,32,256]{3,2,1,0:T(8,128)S(1)}, u32[]{:S(2)}, u32[]{:S(2)}) collective-permute-start(f32[2,2,32,256]{3,2,1,0:T(8,128)S(1)} %get-tuple-element.197), channel_id=1, source_target_pairs={{8,0},{16,8},{24,16},{9,1},{17,9},{25,17},{10,2},{18,10},{26,18},{... | collective-permute-start | bytes 393224 | tf_op jit(solution)/shard_map/ppermute | solution.py:26
  419.5 9.2 %collective-permute-start.40 = (f32[2,4,1,256]{3,2,1,0:T(1,128)S(1)}, f32[2,4,1,256]{3,2,1,0:T(1,128)S(1)}, u32[]{:S(2)}, u32[]{:S(2)}) collective-permute-start(f32[2,4,1,256]{3,2,1,0:T(1,128)S(1)} %get-tuple-element.194), channel_id=1, source_target_pairs={{1,0},{2,1},{3,2},{4,3},{5,4},{6,5},{7,6},{9,8},{10,9},{11,10},{12... | collective-permute-start | bytes 24584 | tf_op jit(solution)/shard_map/ppermute | solution.py:26
  420.8 7.9 collective-permute-start.41
  424.7 252.4 %all-to-all-start = ((f32[8,2,2]{2,1,0:T(2,128)}), f32[8,2,2]{2,1,0:T(2,128)S(1)}, u32[]{:S(2)}, u32[]{:S(2)}) async-start(f32[8,2,2]{2,1,0:T(2,128)} %bitcast.43), calls=%async_computation | async-start | bytes 16384 | tf_op jit(solution)/shard_map/all_to_all | solution.py:127
  462.7 8.9 %collective-permute-start.46 = (f32[2,2,32,256]{3,2,1,0:T(8,128)S(1)}, f32[2,2,32,256]{3,2,1,0:T(8,128)S(1)}, u32[]{:S(2)}, u32[]{:S(2)}) collective-permute-start(f32[2,2,32,256]{3,2,1,0:T(8,128)S(1)} %get-tuple-element.192), channel_id=1, source_target_pairs={{0,8},{8,16},{16,24},{1,9},{9,17},{17,25},{2,10},{10,18},{18,26},{... | collective-permute-start | bytes 393224 | tf_op jit(solution)/shard_map/ppermute | solution.py:25
  465.1 6.9 collective-permute-start.47
  466.4 4.9 collective-permute-start.44
  467.7 3.8 collective-permute-start.45
  502.4 9.1 %collective-permute-start.50 = (f32[2,2,32,256]{3,2,1,0:T(8,128)S(1)}, f32[2,2,32,256]{3,2,1,0:T(8,128)S(1)}, u32[]{:S(2)}, u32[]{:S(2)}) collective-permute-start(f32[2,2,32,256]{3,2,1,0:T(8,128)S(1)} %get-tuple-element.188), channel_id=1, source_target_pairs={{0,8},{8,16},{16,24},{1,9},{9,17},{17,25},{2,10},{10,18},{18,26},{... | collective-permute-start | bytes 393224 | tf_op jit(solution)/shard_map/ppermute | solution.py:25
  505.0 6.9 collective-permute-start.51
  506.4 5.0 collective-permute-start.48
  507.7 3.8 collective-permute-start.49
  542.2 9.0 %collective-permute-start.54 = (f32[2,2,32,256]{3,2,1,0:T(8,128)S(1)}, f32[2,2,32,256]{3,2,1,0:T(8,128)S(1)}, u32[]{:S(2)}, u32[]{:S(2)}) collective-permute-start(f32[2,2,32,256]{3,2,1,0:T(8,128)S(1)} %get-tuple-element.184), channel_id=1, source_target_pairs={{0,8},{8,16},{16,24},{1,9},{9,17},{17,25},{2,10},{10,18},{18,26},{... | collective-permute-start | bytes 393224 | tf_op jit(solution)/shard_map/ppermute | solution.py:25
  544.7 6.9 collective-permute-start.55
  546.0 5.0 collective-permute-start.52
  581.8 9.1 %collective-permute-start.58 = (f32[2,2,32,256]{3,2,1,0:T(8,128)S(1)}, f32[2,2,32,256]{3,2,1,0:T(8,128)S(1)}, u32[]{:S(2)}, u32[]{:S(2)}) collective-permute-start(f32[2,2,32,256]{3,2,1,0:T(8,128)S(1)} %get-tuple-element.180), channel_id=1, source_target_pairs={{0,8},{8,16},{16,24},{1,9},{9,17},{17,25},{2,10},{10,18},{18,26},{... | collective-permute-start | bytes 393224 | tf_op jit(solution)/shard_map/ppermute | solution.py:25
  584.4 6.9 collective-permute-start.59
  585.7 4.9 collective-permute-start.56
  621.5 9.0 %collective-permute-start.62 = (f32[2,2,32,256]{3,2,1,0:T(8,128)S(1)}, f32[2,2,32,256]{3,2,1,0:T(8,128)S(1)}, u32[]{:S(2)}, u32[]{:S(2)}) collective-permute-start(f32[2,2,32,256]{3,2,1,0:T(8,128)S(1)} %get-tuple-element.176), channel_id=1, source_target_pairs={{0,8},{8,16},{16,24},{1,9},{9,17},{17,25},{2,10},{10,18},{18,26},{... | collective-permute-start | bytes 393224 | tf_op jit(solution)/shard_map/ppermute | solution.py:25
  623.9 6.9 collective-permute-start.63
  625.3 5.0 collective-permute-start.60
  677.1 10.9 %all-to-all-start.1 = ((f32[8,2,2]{1,2,0:T(2,128)}), f32[8,2,2]{1,2,0:T(2,128)S(1)}, u32[]{:S(2)}, u32[]{:S(2)}) async-start(f32[8,2,2]{1,2,0:T(2,128)} %copy.34), calls=%async_computation.1 | async-start | bytes 16384 | tf_op jit(solution)/shard_map/all_to_all | solution.py:126
  688.0 99.3 %all-to-all-start.2 = ((f32[8,2,256,256]{3,2,1,0:T(8,128)}), f32[8,2,256,256]{3,2,1,0:T(8,128)}, u32[]{:S(2)}, u32[]{:S(2)}) async-start(f32[8,2,256,256]{3,2,1,0:T(8,128)} %copy.36), calls=%async_computation.2 | async-start | bytes 8388608 | tf_op jit(solution)/shard_map/all_to_all | solution.py:125
  (10 other events, 565.2 us)
